TPU v7x, 512 devices: a whole 4x4x16 slice. The times are simulated.
512 devices in a mesh: seq: 64 (over y, z), exp: 8 (over x, core).
Axes of the slice: x: 4, y: 4, z: 16, core: 2. Of those that a mesh axis runs over, the one named last changes fastest.
Arguments:
- tokens: bfloat16 [4096, 128], P('seq'), may hold values from -36 to 36
- norm_gains: float32 [2, 4096], P(None, 'seq'), may hold values from 0.1 to 1.9
- q_weight: bfloat16 [4096, 4096], P('seq', 'exp'), may hold values from -16 to 16
- kv_weight: bfloat16 [4096, 2, 1024], P('seq', None, 'exp'), may hold values from -1 to 1
- out_weight: bfloat16 [4096, 4096], P('seq', 'exp'), may hold values from -0.3 to 0.3
- kv_cache: bfloat16 [2, 512, 256, 1024], P(None, 'seq', None, 'exp'), may hold values from -8 to 8
- block_count: int32 [32], replicated, may hold values from 1 to 128, 512 in all
- placement: int32 [512], P('seq'), may hold values from 0 to 511, each once
- block_live: int32 [512], P('seq'), may hold values 0 or 1
- router_weight: bfloat16 [4096, 8], P('seq'), may hold values from -0.09375 to 0.09375
- routes: int32 [128, 2], replicated, may hold values from 0 to 7, all different within a row
- expert_in: bfloat16 [8, 2, 4096, 7168], P(None, None, 'seq', 'exp'), may hold values from -0.09375 to 0.09375
- expert_out: bfloat16 [8, 4096, 7168], P(None, 'seq', 'exp'), may hold values from -0.0625 to 0.0625
Outputs:
- layer_out: bfloat16 [4096, 128], P('seq')
Inputs may be any that keep to these rules, and one draw needn't show every extreme that they name: `block_count`: the counts sum to 512; the longest request holds exactly 128 blocks. `placement`: each pool slot holds a different block. `routes`: each row names two different experts.
All inputs are finite; a program needn't handle non-finite values. No bound on the sum of `block_live` on one device may be relied on, other than what follows from the above.
Results may differ from a plain program's by a relative error of at most 0.0065.
Values may be sent and summed in bfloat16 or wider, within the bound.
A program may use at most 128 MiB of HBM per device.

v0:
```python
import math

import jax
import jax.numpy as jnp
from jax import lax
from jax.sharding import PartitionSpec as P

D = 4096
HEAD_DIM = 128
TOPK = 2


NEGATIVE = -1e30
EPSILON = 1e-05


def block_owners(block_count, placement):
    starts = jnp.cumsum(block_count) - block_count
    before = (starts[None, :] <= placement[:, None]).astype(jnp.int32)
    return jnp.sum(before, axis=1) - 1


def softmax_join(first_part, second_part):
    joined_top = jnp.maximum(first_part[0], second_part[0])
    first_factor = jnp.exp(first_part[0] - joined_top)
    second_factor = jnp.exp(second_part[0] - joined_top)
    joined_total = first_part[1] * first_factor + second_part[1] * second_factor
    joined_sum = first_part[2] * first_factor[..., None] + second_part[2] * second_factor[..., None]
    return (joined_top, joined_total, joined_sum)


def per_device(
    tokens,
    norm_gains,
    q_weight,
    kv_weight,
    out_weight,
    kv_cache,
    block_count,
    placement,
    block_live,
    router_weight,
    routes,
    expert_in,
    expert_out,
):
    width_dev, row_total = tokens.shape
    requests = block_count.shape[0]
    steps_all = row_total // requests
    kv_heads_dev = kv_cache.shape[3] // HEAD_DIM
    heads_dev = q_weight.shape[1] // HEAD_DIM
    group_size = heads_dev // kv_heads_dev
    blocks_dev = kv_cache.shape[1]
    page_rows = kv_cache.shape[2]
    experts_all = expert_in.shape[0]
    ff_dev = expert_in.shape[3]
    score_scale = 1.0 / math.sqrt(HEAD_DIM)
    contract_first = (((0,), (0,)), ((), ()))
    token_float = tokens.astype(jnp.float32)
    normed = (token_float * norm_gains[0][:, None]).astype(jnp.bfloat16)
    query_part = lax.dot_general(
        normed, q_weight, contract_first, preferred_element_type=jnp.float32
    )
    fresh_part = lax.dot_general(
        normed, kv_weight.reshape(width_dev, -1), contract_first, preferred_element_type=jnp.float32
    )
    first_local = jnp.sum(token_float * token_float, axis=0)
    query_sum, fresh_sum, first_squares = lax.psum((query_part, fresh_part, first_local), "seq")
    attn_rms = lax.rsqrt(first_squares / D + EPSILON)
    queries = (
        (query_sum * attn_rms[:, None])
        .astype(jnp.bfloat16)
        .reshape(steps_all, requests, kv_heads_dev, group_size, HEAD_DIM)
    )
    fresh_rows = (
        (fresh_sum * attn_rms[:, None])
        .astype(jnp.bfloat16)
        .reshape(steps_all, requests, 2, kv_heads_dev, HEAD_DIM)
    )
    new_keys = fresh_rows[:, :, 0]
    new_values = fresh_rows[:, :, 1]
    cache_keys = kv_cache[0].reshape(blocks_dev, page_rows, kv_heads_dev, HEAD_DIM)
    cache_values = kv_cache[1].reshape(blocks_dev, page_rows, kv_heads_dev, HEAD_DIM)
    block_owner = block_owners(block_count, placement)
    block_alive = (block_live == 1)[:, None, None, None]
    member = (block_owner[:, None] == jnp.arange(requests)[None, :])[:, :, None, None, None]

    def attend(query_steps, first_step):
        step_count = query_steps.shape[0]
        picked = query_steps[:, block_owner]
        scores = (
            jnp.einsum("tpkgd,pjkd->pkgtj", picked, cache_keys, preferred_element_type=jnp.float32)
            * score_scale
        )
        block_top = jnp.max(scores, axis=-1)
        weights = jnp.exp(scores - block_top[..., None]).astype(jnp.bfloat16)
        block_total = jnp.sum(weights, axis=-1, dtype=jnp.float32)
        block_sum = jnp.einsum(
            "pkgtj,pjkd->pkgtd", weights, cache_values, preferred_element_type=jnp.float32
        )
        block_top = jnp.where(block_alive, block_top, NEGATIVE)
        block_total = jnp.where(block_alive, block_total, 0.0)
        block_sum = jnp.where(block_alive[..., None], block_sum, 0.0)
        local_top = jnp.max(jnp.where(member, block_top[:, None], NEGATIVE), axis=0)
        factor = jnp.where(
            member, jnp.exp(jnp.where(member, block_top[:, None] - local_top[None], NEGATIVE)), 0.0
        )
        local_total = jnp.sum(factor * block_total[:, None], axis=0)
        local_sum = jnp.einsum(
            "prkgt,pkgtd->rkgtd", factor, block_sum, precision=lax.Precision.HIGHEST
        )
        whole_top = lax.pmax(local_top, "seq")
        rescale = jnp.exp(local_top - whole_top)
        whole_total, whole_sum = lax.psum(
            (local_total * rescale, local_sum * rescale[..., None]), "seq"
        )
        new_scores = (
            jnp.einsum(
                "trkgd,srkd->rkgts", query_steps, new_keys, preferred_element_type=jnp.float32
            )
            * score_scale
        )
        causal = (first_step + jnp.arange(step_count))[:, None] >= jnp.arange(steps_all)[None, :]
        new_scores = jnp.where(causal, new_scores, NEGATIVE)
        new_top = jnp.max(new_scores, axis=-1)
        new_weights = jnp.where(causal, jnp.exp(new_scores - new_top[..., None]), 0.0).astype(
            jnp.bfloat16
        )
        new_total = jnp.sum(new_weights, axis=-1, dtype=jnp.float32)
        new_sum = jnp.einsum(
            "rkgts,srkd->rkgtd", new_weights, new_values, preferred_element_type=jnp.float32
        )
        joined_top, joined_total, joined_sum = softmax_join(
            (whole_top, whole_total, whole_sum), (new_top, new_total, new_sum)
        )
        attended = (joined_sum / joined_total[..., None]).astype(jnp.bfloat16)
        return jnp.transpose(attended, (3, 0, 1, 2, 4)).reshape(
            step_count * requests, heads_dev * HEAD_DIM
        )

    attention = jnp.concatenate(
        [
            attend(queries[step_index : step_index + 1], step_index)
            for step_index in range(steps_all)
        ],
        axis=0,
    )
    head_part = lax.dot_general(
        out_weight, attention, (((1,), (1,)), ((), ())), preferred_element_type=jnp.float32
    )
    residual = token_float + lax.psum(head_part, "exp")
    second_local = jnp.sum(residual * residual, axis=0)
    hidden_in = (residual * norm_gains[1][:, None]).astype(jnp.bfloat16)
    router_part = lax.dot_general(
        router_weight, hidden_in, contract_first, preferred_element_type=jnp.float32
    )
    expert_ids = jnp.arange(experts_all)
    chosen_part = jnp.sum(
        jnp.where(routes[:, :, None] == expert_ids[None, None, :], router_part.T[:, None, :], 0.0),
        axis=2,
    )
    flat_routes = routes.reshape(-1)
    pair_rows = row_total * TOPK
    second_squares, logit_sums = lax.psum((second_local, chosen_part), "seq")
    moe_rms = lax.rsqrt(second_squares / D + EPSILON)
    share_rows = pair_rows // lax.axis_size("seq")
    chosen = routes
    every_expert = lax.dot_general(
        hidden_in, expert_in, (((0,), (2,)), ((), ())), preferred_element_type=jnp.float32
    )
    one_hot = (chosen[:, :, None] == expert_ids[None, None, :]).astype(jnp.float32)
    result = jnp.einsum("ike,iecf->ikcf", one_hot, every_expert, precision=lax.Precision.HIGHEST)
    inputs = lax.psum_scatter(
        result.reshape(lax.axis_size("seq") * share_rows, 2 * ff_dev),
        "seq",
        scatter_dimension=0,
        tiled=True,
    )
    share_scale = lax.dynamic_slice_in_dim(
        jnp.repeat(moe_rms, TOPK), lax.axis_index("seq") * share_rows, share_rows, 0
    )
    inputs = inputs * share_scale[:, None]
    chosen = flat_routes
    product = lax.dot_general(
        expert_out,
        lax.all_gather(
            (jax.nn.silu(inputs[:, :ff_dev]) * inputs[:, ff_dev:]).astype(jnp.bfloat16),
            "seq",
            axis=0,
            tiled=True,
        ),
        (((2,), (1,)), ((), ())),
        preferred_element_type=jnp.float32,
    )
    picked = chosen[None, :] == expert_ids[:, None]
    expert_rows = jnp.sum(jnp.where(picked[:, None, :], product, 0.0), axis=0)
    logits = logit_sums * moe_rms[:, None]
    sigmoids = jax.nn.sigmoid(logits)
    gate_weights = sigmoids / jnp.sum(sigmoids, axis=1, keepdims=True)
    expert_part = jnp.sum(
        expert_rows.reshape(width_dev, row_total, TOPK) * gate_weights[None], axis=2
    )
    expert_total = lax.psum(expert_part.astype(jnp.bfloat16), "exp").astype(jnp.float32)
    return (residual + expert_total).astype(jnp.bfloat16)


def solution(mesh):
    return jax.shard_map(
        per_device,
        mesh=mesh,
        in_specs=(
            P("seq", None),
            P(None, "seq"),
            P("seq", "exp"),
            P("seq", None, "exp"),
            P("seq", "exp"),
            P(None, "seq", None, "exp"),
            P(),
            P("seq"),
            P("seq"),
            P("seq", None),
            P(),
            P(None, None, "seq", "exp"),
            P(None, "seq", "exp"),
        ),
        out_specs=P("seq", None),
        check_vma=False,
    )
```

profile of v0, /device:TPU:1, one launch (start us, length us, event | category | flops | bytes accessed | tf_op | source)
XLA Modules:
  0.0 1135.4 jit_solution(5942021511305152113)
XLA Ops:
  7.4 1.9 fusion.120
  12.5 122.9 %psum.106 = f32[128]{0:T(128)S(1)} all-reduce(f32[128]{0:T(128)S(1)} %fusion.58), channel_id=1, replica_groups=mesh['seq'=64,'exp'=8] {'seq'}, use_global_device_ids=true, to_apply=%region_2.0 | all-reduce | flops 128 | bytes 1024 | tf_op jit(solution)/shard_map/psum | solution.py:68
  136.9 1.7 fusion.59
  138.6 133.2 %all-reduce.9.cloned.1.call-done = f32[128,512]{1,0:T(8,128)} async-done(((f32[128,512]{1,0:T(8,128)}), f32[128,512]{1,0:T(8,128)}) %all-reduce.9.cloned.1.call-update) | async-done | bytes 262160 | tf_op jit(solution)/shard_map/psum | solution.py:68
  271.8 1.0 multiply_convert_fusion
  274.1 1.3 fusion.162
  280.0 114.7 %all-reduce.4 = (f32[32,1,4,1]{0,2,3,1:T(4,128)S(1)}, f32[32,1,4,1]{0,2,3,1:T(4,128)S(1)}, f32[32,1,4,1]{0,2,3,1:T(4,128)S(1)}, f32[32,1,4,1]{0,2,3,1:T(4,128)S(1)}) all-reduce(f32[32,1,4,1]{0,2,3,1:T(4,128)S(1)} %bitcast.383, f32[32,1,4,1]{0,2,3,1:T(4,128)S(1)} %bitcast.389, ...), channel_id=1, replica_groups=mesh['seq'=64,'exp'=8] {'seq'}, use_global_device_ids=true, to_apply=%region_35.36 | all-reduce | flops 512 | bytes 4096 | tf_op jit(solution)/shard_map/pmax | solution.py:112
  394.8 1.0 fusion.5
  395.8 1.0 fusion.7
  396.8 1.0 fusion.9
  397.8 1.0 fusion.11
  398.9 113.0 %all-reduce.2 = (f32[32,1,4,1]{0,2,3,1:T(4,128)S(1)}, f32[32,1,4,1]{0,2,3,1:T(4,128)S(1)}, f32[32,1,4,1]{0,2,3,1:T(4,128)S(1)}, f32[32,1,4,1]{0,2,3,1:T(4,128)S(1)}) all-reduce(f32[32,1,4,1]{0,2,3,1:T(4,128)S(1)} %get-tuple-element.62, f32[32,1,4,1]{0,2,3,1:T(4,128)S(1)} %get-tuple-element.60, ...), channel_id=1, replica_groups=mesh['seq'=64,'exp'=8] {'seq'}, use_global_device_ids=true, to_apply=%region_40.41 | all-reduce | flops 512 | bytes 4096 | tf_op jit(solution)/shard_map/psum | solution.py:114
  511.9 170.3 %all-reduce.13.cloned.1.call-done = (f32[128,256]{1,0:T(8,128)}, f32[32,1,4,1,128]{4,0,2,3,1:T(8,128)}, f32[32,1,4,1,128]{4,0,2,3,1:T(8,128)}, f32[32,1,4,1,128]{4,0,2,3,1:T(8,128)}, f32[32,1,4,1,128]{4,0,2,3,1:T(8,128)}) async-done(((f32[128,256]{1,0:T(8,128)}, f32[32,1,4,1,128]{4,0,2,3,1:T(8,128)}, f32[32,1,4,1,128]{4,0,2,3,1:T(8,128)}, f32[32,1,4,1,128]{4,0,2,3,1:T(8,128)}, ...) | async-done | bytes 393232 | tf_op jit(solution)/shard_map/psum | solution.py:68
  682.3 1.0 multiply_convert_fusion.1
  688.1 31.8 %psum.116 = f32[64,128]{1,0:T(8,128)S(1)} all-reduce(f32[64,128]{1,0:T(8,128)S(1)} %convolution_bitcast_fusion.5), channel_id=1, replica_groups=mesh['seq'=64,'exp'=8] {'exp'}, use_global_device_ids=true, to_apply=%region_42.43 | all-reduce | flops 8192 | bytes 65536 | tf_op jit(solution)/shard_map/psum | solution.py:151
  720.0 1.1 fusion.70
  721.2 6.5 fusion
  728.7 1.3 copy.269
  730.2 1.3 dynamic-slice
  732.8 112.7 %all-reduce.1 = (f32[128]{0:T(128)S(1)}, f32[128,2]{0,1:T(2,128)S(1)}) all-reduce(f32[128]{0:T(128)S(1)} %get-tuple-element.42, f32[128,2]{0,1:T(2,128)S(1)} %copy.252), channel_id=1, replica_groups=mesh['seq'=64,'exp'=8] {'seq'}, use_global_device_ids=true, to_apply=%region_45.46 | all-reduce | flops 384 | bytes 3072 | tf_op jit(solution)/shard_map/psum | solution.py:164
  846.0 149.8 %all-reduce.11.cloned.1.call-done = f32[256,1792]{1,0:T(8,128)} async-done(((f32[256,1792]{1,0:T(8,128)}), f32[256,1792]{1,0:T(8,128)}) %all-reduce.11.cloned.1.call-update) | async-done | bytes 1835024
  996.6 73.2 %all-gather = bf16[64,4,896]{2,1,0:T(4,128)(2,1)S(1)} all-gather(bf16[1,4,896]{2,1,0:T(4,128)(2,1)S(1)} %fusion.118), channel_id=1, replica_groups=mesh['seq'=64,'exp'=8] {'seq'}, dimensions={0}, use_global_device_ids=true | all-gather | bytes 465920 | tf_op jit(solution)/shard_map/all_gather | solution.py:186
  1070.0 1.7 fusion.3
  1072.1 56.1 %psum.119 = bf16[64,128]{1,0:T(8,128)(2,1)S(1)} all-reduce(bf16[64,128]{1,0:T(8,128)(2,1)S(1)} %copy.254), channel_id=1, replica_groups=mesh['seq'=64,'exp'=8] {'exp'}, use_global_device_ids=true, to_apply=%region_51.52 | all-reduce | flops 8192 | bytes 32768 | tf_op jit(solution)/shard_map/psum | solution.py:203
  (136 shorter events, 20.4 us)
Async XLA Ops:
  6.5 713.5 %copy-start = (bf16[8,2,64,896]{3,2,1,0:T(8,128)(2,1)S(1)}, bf16[8,2,64,896]{3,2,1,0:T(8,128)(2,1)}, u32[]{:S(2)}) copy-start(bf16[8,2,64,896]{3,2,1,0:T(8,128)(2,1)} %param.24) | copy-start | bytes 5505028
  6.5 268.9 %copy-start.1 = (bf16[2,8,256,128]{3,2,1,0:T(8,128)(2,1)S(1)}, bf16[2,8,256,128]{3,2,1,0:T(8,128)(2,1)}, u32[]{:S(2)}) copy-start(bf16[2,8,256,128]{3,2,1,0:T(8,128)(2,1)} %param.18) | copy-start | bytes 3145732
  6.5 265.3 %all-reduce.9.cloned.1.call-start = ((), (), s32[]{:S(2)}) async-start(), calls=%async_computation | async-start | bytes 524288 | tf_op jit(solution)/shard_map/psum | solution.py:68
  9.3 673.0 %all-reduce.13.cloned.1.call-start = ((), (), s32[]{:S(2)}) async-start(), calls=%async_computation.2 | async-start | bytes 786432 | tf_op jit(solution)/shard_map/psum | solution.py:68
  398.8 596.9 %all-reduce.11.cloned.1.call-start = ((), (), s32[]{:S(2)}) async-start(), calls=%async_computation.1 | async-start | bytes 3670016
  682.3 3.7 copy-start.5
  682.3 4.6 copy-start.4
  683.3 4.5 copy-start.3
  683.4 4.5 copy-start.7
  683.9 36.0 %copy-start.2 = (bf16[64,128]{1,0:T(8,128)(2,1)S(1)}, bf16[64,128]{1,0:T(8,128)(2,1)}, u32[]{:S(2)}) copy-start(bf16[64,128]{1,0:T(8,128)(2,1)} %param.13) | copy-start | bytes 49156
  730.0 2.1 copy-start.6
Sparse Core Ops, SparseCore 0:
  10.8 261.0 all-reduce.8
  398.9 283.2 all-reduce.12
  730.2 265.5 all-reduce.10
where the time goes:
time: 1140 us
  blocking collectives  625 us (55%)
  waiting for transfers between devices  453 us (40%)
  matrix products  22.1 us (2%)
  between operations  14.3 us (1%)
    psum x2, waiting for transfers between devices, per_device(): lax.psum((query_part, fresh_part, first_local), 'seq')  304 us
    unnamed x4, waiting for transfers between devices  150 us
    psum x1, blocking collectives, per_device(): lax.psum((query_part, fresh_part, first_local), 'seq')  123 us
    pmax x1, blocking collectives, attend(): whole_top = lax.pmax(local_top, 'seq')  115 us
    psum x1, blocking collectives, attend(): lax.psum((local_total * rescale, local_sum * rescale[..., None]), 'seq')  113 us
    psum x1, blocking collectives, per_device(): second_squares, logit_sums = lax.psum((second_local, chosen_part), 'seq')  113 us
    all_gather x1, blocking collectives, per_device(): lax.all_gather((jax.nn.silu(inputs[:, :ff_dev]) * inputs[:, ff_dev:]).ast...  73.2 us
    psum x1, blocking collectives, per_device(): lax.psum(expert_part.astype(jnp.bfloat16), 'exp').astype(jnp.float32)  56.1 us
  transfers between devices with their start and end apart: 3, of which 3 were waited for; matrix products, arithmetic and copies ran while one was open for 1% of the time, Pallas kernels for 0%

commit v1 on v0

v1 whole, which is shorter than its diff:
```python
import functools
import math

import jax
import jax.numpy as jnp
from jax import lax
from jax.experimental import pallas as pl
from jax.experimental.pallas import tpu as pltpu
from jax.sharding import PartitionSpec as P

HEAD_DIM = 128
TOPK = 2
LANES = 128
NEGATIVE = -1e30
EPSILON = 1e-05
MESH = pl.DeviceIdType.MESH
HIGHEST = lax.Precision.HIGHEST
FIRST = (((0,), (0,)), ((), ()))
LAST = (((1,), (1,)), ((), ()))
F32 = jnp.float32
BF16 = jnp.bfloat16


def dot(first, second, dims, precision=None):
    return lax.dot_general(
        first, second, dims, precision=precision, preferred_element_type=F32
    )


def ring_order(count):
    return sorted(range(1, count), key=lambda d: -min(d, count - d))


def kernel(
    cfg,
    same_ref,
    live_ref,
    tok_ref,
    gains_ref,
    qw_ref,
    kvw_ref,
    ow_ref,
    cache_ref,
    sel_ref,
    lead_ref,
    router_ref,
    routes_ref,
    onehot_ref,
    ein_ref,
    eout_ref,
    out_ref,
    a_sy,
    a_ry,
    a_sz,
    a_rz,
    a_g,
    e_sy,
    e_ry,
    e_sz,
    e_rz,
    e_g,
    b_sy,
    b_ry,
    b_sz,
    b_rz,
    b_g,
    x_s1,
    x_r1,
    x_s2,
    x_r2,
    y_send,
    z_send,
    x_send,
    y_recv,
    z_recv,
    x_recv,
):
    ny, nz, nx, depth, steps = cfg
    rows = tok_ref.shape[1]
    ry = rows // ny
    rp = ry // nz
    heads = qw_ref.shape[1] // HEAD_DIM
    qcols = heads * HEAD_DIM
    kcols = qcols + HEAD_DIM
    vcols = kcols + HEAD_DIM
    blocks = cache_ref.shape[1]
    experts = ein_ref.shape[0]
    ff = ein_ref.shape[3]
    scale = 1.0 / math.sqrt(HEAD_DIM)
    seq = lax.axis_index("seq")
    e = lax.axis_index("exp")
    y = lax.div(seq, nz)
    z = lax.rem(seq, nz)

    def y_peer(d):
        return lax.rem(y + d, ny)

    def z_peer(d):
        return lax.rem(z + d, nz)

    def x_peer(d):
        return lax.rem(e + d, nx)

    def y_copy(src, dst, d, phase):
        return pltpu.make_async_remote_copy(
            src_ref=src,
            dst_ref=dst,
            send_sem=y_send.at[d - 1],
            recv_sem=y_recv.at[phase, d - 1],
            device_id=(y_peer(d) * nz + z, e),
            device_id_type=MESH,
        )

    def z_copy(src, dst, d, phase):
        return pltpu.make_async_remote_copy(
            src_ref=src,
            dst_ref=dst,
            send_sem=z_send.at[d - 1],
            recv_sem=z_recv.at[phase, d - 1],
            device_id=(y * nz + z_peer(d), e),
            device_id_type=MESH,
        )

    def run(copies):
        for copy in copies:
            copy.start()
        for copy in copies:
            copy.wait()

    def y_exchange(send, recv, phase):
        recv[y] = send[y]
        run([y_copy(send.at[y_peer(d)], recv.at[y], d, phase) for d in ring_order(ny)])

    def z_exchange(send, recv, phase):
        recv[z] = send[z]
        run([z_copy(send.at[z_peer(d)], recv.at[z], d, phase) for d in ring_order(nz)])

    def gather(held, phase):
        run([z_copy(held.at[y, z], held.at[y, z], d, phase) for d in ring_order(nz)])
        run([y_copy(held.at[y], held.at[y], d, phase) for d in ring_order(ny)])

    def x_reduce(part, send, recv, phase):
        send[...] = part.astype(BF16)
        recv[e] = part.astype(BF16)
        run(
            [
                pltpu.make_async_remote_copy(
                    src_ref=send,
                    dst_ref=recv.at[e],
                    send_sem=x_send.at[d - 1],
                    recv_sem=x_recv.at[phase, d - 1],
                    device_id=(seq, x_peer(d)),
                    device_id_type=MESH,
                )
                for d in ring_order(nx)
            ]
        )
        total = recv[0].astype(F32)
        for index in range(1, nx):
            total = total + recv[index].astype(F32)
        return total

    barrier = pltpu.get_barrier_semaphore()
    for d in range(1, ny):
        pl.semaphore_signal(barrier, inc=1, device_id=(y_peer(d) * nz + z, e), device_id_type=MESH)
    for d in range(1, nz):
        pl.semaphore_signal(barrier, inc=1, device_id=(y * nz + z_peer(d), e), device_id_type=MESH)
    for d in range(1, nx):
        pl.semaphore_signal(barrier, inc=1, device_id=(seq, x_peer(d)), device_id_type=MESH)

    def lane_of(count):
        return lax.broadcasted_iota(jnp.int32, (count, LANES), 1)

    def by_head(columns):
        count = columns[0].shape[0]
        lane = lax.rem(lane_of(count), heads)
        spread = jnp.broadcast_to(columns[0], (count, LANES))
        for h in range(1, heads):
            spread = jnp.where(lane == h, columns[h], spread)
        return spread

    def pack_stats(top, total):
        group = lax.div(lane_of(top.shape[0]), heads)
        high = top.astype(BF16).astype(F32)
        rest = top - high
        middle = rest.astype(BF16).astype(F32)
        total_high = total.astype(BF16).astype(F32)
        packed = jnp.where(group == 0, high, total - total_high)
        packed = jnp.where(group == 1, middle, packed)
        packed = jnp.where(group == 2, rest - middle, packed)
        packed = jnp.where(group == 3, total_high, packed)
        return packed.astype(BF16)

    def stat(values, group, h):
        lane = qcols + group * heads + h
        return values[..., lane : lane + 1]

    def unpack(values, h):
        top = (stat(values, 0, h) + stat(values, 1, h)) + stat(values, 2, h)
        total = stat(values, 3, h) + stat(values, 4, h)
        return top, total, values[..., h * HEAD_DIM : (h + 1) * HEAD_DIM]

    tok = tok_ref[...].astype(F32)
    ones = jnp.ones((tok.shape[0], LANES), F32)
    normed = (tok * gains_ref[:, 0:1]).astype(BF16)
    q_part = dot(normed, qw_ref[...], FIRST)
    kv_part = dot(normed, kvw_ref[...], FIRST)
    squares = dot(tok * tok, ones, FIRST, HIGHEST)
    for part in range(ny):
        here = slice(part * ry, (part + 1) * ry)
        a_sy[part, :, 0:qcols] = q_part[here].astype(BF16)
        a_sy[part, :, qcols:vcols] = kv_part[here].astype(BF16)
        a_sy[part, :, vcols : vcols + LANES] = squares[here].astype(BF16)

    pl.semaphore_wait(barrier, (ny - 1) + (nz - 1) + (nx - 1))
    y_exchange(a_sy, a_ry, 0)
    part_sum = a_ry[0].astype(F32)
    for part in range(1, ny):
        part_sum = part_sum + a_ry[part].astype(F32)
    a_sz[...] = part_sum.reshape(nz, rp, part_sum.shape[1]).astype(BF16)
    z_exchange(a_sz, a_rz, 0)
    fresh = jnp.sum(a_rz[...].astype(F32), axis=0)
    attn_rms = lax.rsqrt(fresh[:, vcols : vcols + 1] / depth + EPSILON)
    own = (fresh[:, 0:vcols] * attn_rms).astype(BF16)
    a_g[y, z] = own
    gather(a_g, 1)
    fresh_rows = a_g[...].astype(F32).reshape(rows, vcols).astype(BF16)

    sel = sel_ref[...]
    picked = [
        dot(sel.astype(BF16), fresh_rows[:, h * HEAD_DIM : (h + 1) * HEAD_DIM], (((1,), (0,)), ((), ())))
        for h in range(heads)
    ]
    tops, totals, sums = [], [], []
    for p in range(blocks):
        here = slice(p * 8, (p + 1) * 8)
        block_query = jnp.concatenate([picked[h][here] for h in range(heads)], axis=0)
        scores = dot(block_query.astype(BF16), cache_ref[0, p], LAST) * scale
        top = jnp.max(scores, axis=1, keepdims=True)
        weights = jnp.exp(scores - top).astype(BF16)
        total = jnp.sum(weights.astype(F32), axis=1, keepdims=True)
        weighted = dot(weights, cache_ref[1, p], (((1,), (0,)), ((), ())))
        alive = live_ref[p]
        top = by_head([top[h * 8 : (h + 1) * 8] for h in range(heads)])
        tops.append(top * alive + (1.0 - alive) * NEGATIVE)
        totals.append(by_head([total[h * 8 : (h + 1) * 8] for h in range(heads)]) * alive)
        sums.append(weighted * alive)
    joint, factors = [], []
    for p in range(blocks):
        best = tops[p]
        for q in range(blocks):
            if q != p:
                best = jnp.maximum(best, tops[q] + same_ref[p * blocks + q])
        joint.append(best)
        factors.append(jnp.exp(tops[p] - best))
    local_total = dot(
        sel, jnp.concatenate([totals[p] * factors[p] for p in range(blocks)], axis=0), FIRST, HIGHEST
    )
    lead = lead_ref[...]
    local_top = dot(lead, jnp.concatenate(joint, axis=0), FIRST, HIGHEST)
    present = dot(lead, jnp.ones((lead.shape[0], LANES), F32), FIRST)
    local_top = jnp.where(present > 0.5, local_top, NEGATIVE)
    local_stats = pack_stats(local_top, local_total)
    local_sums = [
        dot(
            sel,
            jnp.concatenate(
                [sums[p][h * 8 : (h + 1) * 8] * factors[p][:, h : h + 1] for p in range(blocks)],
                axis=0,
            ),
            FIRST,
            HIGHEST,
        )
        for h in range(heads)
    ]
    for part in range(ny):
        here = slice(part * ry, (part + 1) * ry)
        for h in range(heads):
            e_sy[part, :, h * HEAD_DIM : (h + 1) * HEAD_DIM] = local_sums[h][here].astype(BF16)
        e_sy[part, :, qcols : qcols + LANES] = local_stats[here]
    y_exchange(e_sy, e_ry, 2)
    parts = [e_ry[part].astype(F32) for part in range(ny)]
    tops, totals = [], []
    for h in range(heads):
        pieces = [unpack(values, h) for values in parts]
        top = functools.reduce(jnp.maximum, [piece[0] for piece in pieces])
        total, weighted = 0.0, 0.0
        for piece in pieces:
            factor = jnp.exp(piece[0] - top)
            total = total + factor * piece[1]
            weighted = weighted + factor * piece[2]
        tops.append(top)
        totals.append(total)
        e_sz[:, :, h * HEAD_DIM : (h + 1) * HEAD_DIM] = weighted.reshape(nz, rp, HEAD_DIM).astype(BF16)
    stats = pack_stats(by_head(tops), by_head(totals)).astype(F32)
    e_sz[:, :, qcols : qcols + LANES] = stats.reshape(nz, rp, LANES).astype(BF16)
    z_exchange(e_sz, e_rz, 2)
    values = e_rz[...].astype(F32)
    own = own.astype(F32)
    new_rows = [a_g[s, z].astype(F32) for s in range(steps)]
    attended = []
    for h in range(heads):
        tops, totals, sums = unpack(values, h)
        top = jnp.max(tops, axis=0)
        factors = jnp.exp(tops - top[None])
        total = jnp.sum(factors * totals, axis=0)
        weighted = jnp.sum(factors * sums, axis=0)
        query = own[:, h * HEAD_DIM : (h + 1) * HEAD_DIM]
        scores = []
        for s in range(steps):
            score = jnp.sum(query * new_rows[s][:, qcols:kcols], axis=1, keepdims=True) * scale
            scores.append(jnp.where(y >= s, score, NEGATIVE))
        new_top = functools.reduce(jnp.maximum, scores)
        joined = jnp.maximum(top, new_top)
        new_total, new_sum = 0.0, 0.0
        for s in range(steps):
            weight = jnp.where(y >= s, jnp.exp(scores[s] - new_top), 0.0)
            weight = weight.astype(BF16).astype(F32)
            new_total = new_total + weight
            new_sum = new_sum + weight * new_rows[s][:, kcols:vcols]
        old_factor = jnp.exp(top - joined)
        new_factor = jnp.exp(new_top - joined)
        total = total * old_factor + new_total * new_factor
        weighted = weighted * old_factor + new_sum * new_factor
        attended.append(weighted / total)
    e_g[y, z] = jnp.concatenate(attended, axis=1).astype(BF16)
    gather(e_g, 3)
    attention = e_g[...].astype(F32).reshape(rows, qcols).astype(BF16)

    head_part = dot(ow_ref[...], attention, LAST)
    residual = tok + x_reduce(head_part, x_s1, x_r1, 0)

    hidden = (residual * gains_ref[:, 1:2]).astype(BF16)
    logits = dot(hidden, router_ref[...], FIRST)
    squares = dot(residual * residual, ones, FIRST, HIGHEST)
    stats = jnp.where(lane_of(rows) < experts, logits, squares).astype(BF16)
    hidden_float = hidden.astype(F32)
    masked = [
        jnp.concatenate(
            [
                jnp.where(routes_ref[k : k + 1, :] == expert, hidden_float, 0.0)
                for expert in range(experts)
            ],
            axis=0,
        )
        for k in range(TOPK)
    ]
    masked = jnp.concatenate(masked, axis=1).astype(BF16)
    for c in range(2):
        weight = ein_ref[:, c].reshape(experts * ein_ref.shape[2], ff)
        product = dot(masked, weight, FIRST)
        for part in range(ny):
            for k in range(TOPK):
                start = k * rows + part * ry
                b_sy[part, k * ry : (k + 1) * ry, c * ff : (c + 1) * ff] = product[
                    start : start + ry
                ].astype(BF16)
    for part in range(ny):
        for k in range(TOPK):
            b_sy[part, k * ry : (k + 1) * ry, 2 * ff : 2 * ff + LANES] = stats[
                part * ry : (part + 1) * ry
            ]
    y_exchange(b_sy, b_ry, 4)
    part_sum = b_ry[0].astype(F32)
    for part in range(1, ny):
        part_sum = part_sum + b_ry[part].astype(F32)
    for k in range(TOPK):
        b_sz[:, k] = part_sum[k * ry : (k + 1) * ry].reshape(nz, rp, part_sum.shape[1]).astype(BF16)
    z_exchange(b_sz, b_rz, 4)
    inputs = [jnp.sum(b_rz[:, k].astype(F32), axis=0) for k in range(TOPK)]
    moe_rms = lax.rsqrt(inputs[0][:, 2 * ff + 64 : 2 * ff + 65] / depth + EPSILON)
    sigmoids = []
    for k in range(TOPK):
        chosen = inputs[0][:, 2 * ff : 2 * ff + LANES] * onehot_ref[seq, k]
        logit = jnp.sum(chosen, axis=1, keepdims=True) * moe_rms
        sigmoids.append(1.0 / (1.0 + jnp.exp(-logit)))
    for k in range(TOPK):
        gate = inputs[k][:, 0:ff] * moe_rms
        up = inputs[k][:, ff : 2 * ff] * moe_rms
        active = gate / (1.0 + jnp.exp(-gate)) * up
        b_g[y, z, k] = (active * (sigmoids[k] / (sigmoids[0] + sigmoids[1]))).astype(BF16)
    gather(b_g, 5)
    expert_part = jnp.zeros(residual.shape, F32)
    for k in range(TOPK):
        active = b_g[:, :, k].astype(F32).reshape(rows, ff).astype(BF16)
        for expert in range(experts):
            product = dot(eout_ref[expert], active, LAST)
            expert_part = expert_part + jnp.where(routes_ref[k : k + 1, :] == expert, product, 0.0)
    out_ref[...] = (residual + x_reduce(expert_part, x_s2, x_r2, 1)).astype(BF16)


def block_owners(block_count, placement):
    starts = jnp.cumsum(block_count) - block_count
    before = (starts[None, :] <= placement[:, None]).astype(jnp.int32)
    return jnp.sum(before, axis=1) - 1


def per_device(
    nx,
    seq_size,
    tokens,
    norm_gains,
    q_weight,
    kv_weight,
    out_weight,
    kv_cache,
    block_count,
    placement,
    block_live,
    router_weight,
    routes,
    expert_in,
    expert_out,
):
    width, rows = tokens.shape
    requests = block_count.shape[0]
    steps = rows // requests
    ny, nz = steps, seq_size // steps
    rp = rows // seq_size
    blocks = kv_cache.shape[1]
    experts, _, _, ff = expert_in.shape
    qcols = q_weight.shape[1]
    vcols = qcols + 2 * HEAD_DIM
    owner = block_owners(block_count, placement)
    step = jnp.arange(8)
    column = jnp.where(step[None, :] < steps, owner[:, None] + step[None, :] * requests, -1)
    sel = column.reshape(-1)[:, None] == jnp.arange(rows)[None, :]
    same = owner[:, None] == owner[None, :]
    earlier = jnp.arange(blocks)[:, None] > jnp.arange(blocks)[None, :]
    leads = jnp.logical_not(jnp.any(same & earlier, axis=1))
    lead = sel & jnp.repeat(leads, 8)[:, None]
    penalty = jnp.where(same, 0.0, NEGATIVE).astype(F32).reshape(-1)
    alive = (block_live == 1).astype(F32)
    onehot = (routes[:, :, None] == jnp.arange(LANES)[None, None, :]).astype(F32)
    onehot = onehot.reshape(seq_size, rp, TOPK, LANES).transpose(0, 2, 1, 3)
    acols, ecols, bcols = vcols + LANES, qcols + LANES, 2 * ff + LANES
    ry = rows // ny
    vmem = pl.BlockSpec(memory_space=pltpu.VMEM)
    smem = pl.BlockSpec(memory_space=pltpu.SMEM)
    return pl.pallas_call(
        functools.partial(kernel, (ny, nz, nx, width * seq_size, steps)),
        out_shape=jax.ShapeDtypeStruct((width, rows), BF16),
        in_specs=[smem, smem] + [vmem] * 13,
        out_specs=vmem,
        scratch_shapes=[
            pltpu.VMEM((ny, ry, acols), BF16),
            pltpu.VMEM((ny, ry, acols), BF16),
            pltpu.VMEM((nz, rp, acols), BF16),
            pltpu.VMEM((nz, rp, acols), BF16),
            pltpu.VMEM((ny, nz, rp, vcols), BF16),
            pltpu.VMEM((ny, ry, ecols), BF16),
            pltpu.VMEM((ny, ry, ecols), BF16),
            pltpu.VMEM((nz, rp, ecols), BF16),
            pltpu.VMEM((nz, rp, ecols), BF16),
            pltpu.VMEM((ny, nz, rp, qcols), BF16),
            pltpu.VMEM((ny, TOPK * ry, bcols), BF16),
            pltpu.VMEM((ny, TOPK * ry, bcols), BF16),
            pltpu.VMEM((nz, TOPK, rp, bcols), BF16),
            pltpu.VMEM((nz, TOPK, rp, bcols), BF16),
            pltpu.VMEM((ny, nz, TOPK, rp, ff), BF16),
            pltpu.VMEM((width, rows), BF16),
            pltpu.VMEM((nx, width, rows), BF16),
            pltpu.VMEM((width, rows), BF16),
            pltpu.VMEM((nx, width, rows), BF16),
            pltpu.SemaphoreType.DMA((ny - 1,)),
            pltpu.SemaphoreType.DMA((nz - 1,)),
            pltpu.SemaphoreType.DMA((nx - 1,)),
            pltpu.SemaphoreType.DMA((6, ny - 1)),
            pltpu.SemaphoreType.DMA((6, nz - 1)),
            pltpu.SemaphoreType.DMA((2, nx - 1)),
        ],
        compiler_params=pltpu.CompilerParams(
            collective_id=0, has_side_effects=True, vmem_limit_bytes=60 * 1024 * 1024
        ),
    )(
        penalty,
        alive,
        tokens,
        norm_gains.T,
        q_weight,
        kv_weight.reshape(width, -1),
        out_weight,
        kv_cache,
        sel.astype(F32),
        lead.astype(F32),
        jnp.pad(router_weight, ((0, 0), (0, LANES - experts))),
        routes.T,
        onehot,
        expert_in,
        expert_out,
    )


def solution(mesh):
    return jax.shard_map(
        functools.partial(per_device, mesh.shape["exp"], mesh.shape["seq"]),
        mesh=mesh,
        in_specs=(
            P("seq", None),
            P(None, "seq"),
            P("seq", "exp"),
            P("seq", None, "exp"),
            P("seq", "exp"),
            P(None, "seq", None, "exp"),
            P(),
            P("seq"),
            P("seq"),
            P("seq", None),
            P(),
            P(None, None, "seq", "exp"),
            P(None, "seq", "exp"),
        ),
        out_specs=P("seq", None),
        check_vma=False,
    )
```

time: 1140 us -> 132 us (0.12)
  blocking collectives: 625 us -> 0 us
  waiting for transfers between devices: 453 us -> 0 us
  Pallas kernels: 0 us -> 119 us
  matrix products: 22.1 us -> 0 us
  between operations: 14.3 us -> 0.04 us
    psum x5 -> x0, blocking collectives: 437 us -> none  [the longest x1 123 us: per_device(): lax.psum((query_part, fresh_part, first_local), 'seq')]
    psum x2 -> x0, waiting for transfers between devices: 304 us -> none  [per_device(): lax.psum((query_part, fresh_part, first_local), 'seq')]
    unnamed x4 -> x0, waiting for transfers between devices: 150 us -> none
    pallas_call x0 -> x1, Pallas kernels: none -> 119 us  [per_device(): pl.pallas_call(functools.partial(kernel, (ny, nz, nx, width * seq_size, s...]
    pmax x1 -> x0, blocking collectives: 115 us -> none  [attend(): whole_top = lax.pmax(local_top, 'seq')]
    all_gather x1 -> x0, blocking collectives: 73.2 us -> none  [per_device(): lax.all_gather((jax.nn.silu(inputs[:, :ff_dev]) * inputs[:, ff_dev:]).ast...]
    dot_general x27 -> x0, matrix products: 22.1 us -> none  [the longest x1 6.55 us: per_device(): jnp.einsum('ike,iecf->ikcf', one_hot, every_expert, precision=lax.Precisi...]
  transfers between devices with their start and end apart: 3 -> 0, of which waited for: 3 -> 0; matrix products, arithmetic and copies ran while one was open for 1% -> 0% of each run, Pallas kernels for 0% -> 0%
where the time goes in v1:
time: 132 us
  Pallas kernels  119 us (90%)
  local copies, waits for them, and re-layouts  7.91 us (6%)
  other arithmetic  4.7 us (4%)
    pallas_call x1, Pallas kernels, per_device(): pl.pallas_call(functools.partial(kernel, (ny, nz, nx, width * seq_size, s...  119 us
    unnamed x4, local copies, waits for them, and re-layouts  4.83 us

profile of v1, /device:TPU:1, one launch (start us, length us, event | category | flops | bytes accessed | tf_op | source)
XLA Modules:
  0.0 131.8 jit_solution(9832331818420981339)
XLA Ops:
  0.0 0.7 copy.22
  0.7 0.1 reduce-window.9
  0.8 0.1 reduce
  0.9 0.7 sub.6
  1.6 0.8 convert_reduce_fusion
  2.4 0.1 add_select_fusion
  2.5 0.1 select_n.22
  2.6 0.2 fusion.3
  2.8 0.1 broadcast_in_dim.39
  2.8 0.1 and.14
  2.9 0.7 fusion.2
  3.7 0.1 compare_select_fusion
  3.7 0.6 select_n.20.same_ref
  4.3 0.8 eq.57
  5.2 0.1 copy.25
  5.2 0.8 compare_convert_fusion.onehot_ref
  6.1 1.4 %copy.23 = f32[2,64]{0,1:T(8,128)} copy(f32[2,64]{1,0:T(2,128)} %param.14) | data formatting | bytes 1024 | tf_op args[1]
  7.4 1.4 %copy.28 = bf16[8,8,2,128]{3,1,2,0:T(8,128)(2,1)} copy(bf16[8,8,2,128]{3,2,1,0:T(2,128)(2,1)} %bitcast.13) | data formatting | bytes 65536
  8.8 0.8 copy.24
  9.6 0.6 pad.4.router_ref
  10.2 1.1 compare_convert_fusion.1.live_ref
  11.3 119.2 %shard_map.127 = bf16[64,128]{1,0:T(8,128)(2,1)} custom-call(f32[64]{0:T(128)} %select_n.20.same_ref, f32[8]{0:T(128)} %compare_convert_fusion.1.live_ref, bf16[64,128]{1,0:T(8,128)(2,1)} %tok_ref.1, f32[64,2]{1,0:T(8,128)} %bitcast.11, bf16[64,512]{1,0:T(8,128)(2,1)} %qw_ref.1, bf16[64,256]{1,0:T(8,128)(2,1)} %bitcast.12, bf16[64,512]{1,0:T(8,128)(2,1)} %ow_ref.1, ...), custom_call_target="tpu_custom_call" | custom-call | tf_op jit(solution)/shard_map/pallas_call | solution.py:440
  130.5 1.3 %copy.30 = bf16[64,128]{1,0:T(8,128)(2,1)} copy(bf16[64,128]{1,0:T(8,128)(2,1)} %shard_map.127) | data formatting | bytes 32768
  (3 shorter events, 0.0 us)

commit v2 on v1

v2 whole, which is shorter than its diff:
```python
import functools
import math

import jax
import jax.numpy as jnp
from jax import lax
from jax.experimental import pallas as pl
from jax.experimental.pallas import tpu as pltpu
from jax.sharding import PartitionSpec as P

HEAD_DIM = 128
TOPK = 2
LANES = 128
NEGATIVE = -1e30
EPSILON = 1e-05
MESH = pl.DeviceIdType.MESH
HIGHEST = lax.Precision.HIGHEST
FIRST = (((0,), (0,)), ((), ()))
LAST = (((1,), (1,)), ((), ()))
MIDDLE = (((1,), (0,)), ((), ()))
F32 = jnp.float32
BF16 = jnp.bfloat16


def dot(first, second, dims, precision=None):
    return lax.dot_general(
        first, second, dims, precision=precision, preferred_element_type=F32
    )


def ring_order(count):
    return sorted(range(1, count), key=lambda d: -min(d, count - d))


def kernel(
    cfg,
    count_ref,
    place_ref,
    live_ref,
    route_ref,
    tok_ref,
    gains_ref,
    qw_ref,
    kvw_ref,
    ow_ref,
    cache_ref,
    router_ref,
    routes_ref,
    ein_ref,
    eout_ref,
    out_ref,
    a_sy,
    a_ry,
    a_sz,
    a_rz,
    a_g,
    e_sy,
    e_ry,
    e_sz,
    e_rz,
    e_g,
    s_sy,
    s_ry,
    s_sz,
    s_rz,
    b_sy,
    b_ry,
    b_sz,
    b_rz,
    b_g,
    x_s,
    x_p,
    x_r,
    y_send,
    z_send,
    x_send,
    y_recv,
    z_recv,
    x_recv,
):
    ny, nz, nx, depth, steps = cfg
    width, rows = tok_ref.shape
    requests = count_ref.shape[0]
    ry = rows // ny
    rp = ry // nz
    heads = qw_ref.shape[1] // HEAD_DIM
    qcols = heads * HEAD_DIM
    kcols = qcols + HEAD_DIM
    vcols = kcols + HEAD_DIM
    blocks = cache_ref.shape[1]
    experts = ein_ref.shape[0]
    ff = ein_ref.shape[3]
    scale = 1.0 / math.sqrt(HEAD_DIM)
    seq = lax.axis_index("seq")
    e = lax.axis_index("exp")
    y = lax.div(seq, nz)
    z = lax.rem(seq, nz)
    chips = nx // 2
    chip = lax.div(e, 2)
    partner = e + 1 - 2 * lax.rem(e, 2)
    started = []

    def y_peer(d):
        return lax.rem(y + d, ny)

    def z_peer(d):
        return lax.rem(z + d, nz)

    def chip_peer(d):
        return lax.rem(e + 2 * d, nx)

    def push(src, dst, send_sem, recv_sem, device):
        copy = pltpu.make_async_remote_copy(
            src_ref=src,
            dst_ref=dst,
            send_sem=send_sem,
            recv_sem=recv_sem,
            device_id=device,
            device_id_type=MESH,
        )
        copy.start()
        started.append(copy)
        return copy

    def y_push(src, dst, d, phase):
        device = (y_peer(d) * nz + z, e)
        return push(src, dst, y_send.at[phase, d - 1], y_recv.at[phase, d - 1], device)

    def z_push(src, dst, d, phase):
        device = (y * nz + z_peer(d), e)
        return push(src, dst, z_send.at[phase, d - 1], z_recv.at[phase, d - 1], device)

    def arrive(copies):
        for copy in copies:
            copy.wait_recv()

    def y_exchange(send, recv, phase):
        return [y_push(send.at[y_peer(d)], recv.at[d - 1], d, phase) for d in ring_order(ny)]

    def z_exchange(send, recv, phase):
        return [z_push(send.at[z_peer(d)], recv.at[d - 1], d, phase) for d in ring_order(nz)]

    def z_gather(held, phase):
        return [z_push(held.at[y, z], held.at[y, z], d, phase) for d in ring_order(nz)]

    def y_gather(held, phase):
        return [y_push(held.at[y], held.at[y], d, phase) for d in ring_order(ny)]

    def gather(held, phase):
        arrive(z_gather(held, phase))
        arrive(y_gather(held, phase))

    def summed(own, recv, copies):
        total = own.astype(F32)
        arrive(copies)
        for slot in range(len(copies)):
            total = total + recv[slot].astype(F32)
        return total

    def x_reduce(part, phase):
        first, second = x_s.at[phase, 0], x_s.at[phase, 1]
        first[...] = part.astype(BF16)
        copy = push(
            first, x_p.at[phase], x_send.at[phase, 0], x_recv.at[phase, 0], (seq, partner)
        )
        copy.wait_recv()
        pair = (first[...].astype(F32) + x_p[phase].astype(F32)).astype(BF16)
        second[...] = pair
        x_r[phase, chip] = pair
        arrive(
            [
                push(
                    second,
                    x_r.at[phase, chip],
                    x_send.at[phase, d],
                    x_recv.at[phase, d],
                    (seq, chip_peer(d)),
                )
                for d in ring_order(chips)
            ]
        )
        total = x_r[phase, 0].astype(F32)
        for index in range(1, chips):
            total = total + x_r[phase, index].astype(F32)
        return total

    barrier = pltpu.get_barrier_semaphore()
    for d in ring_order(nz):
        pl.semaphore_signal(barrier, inc=1, device_id=(y * nz + z_peer(d), e), device_id_type=MESH)
    for d in range(1, ny):
        pl.semaphore_signal(barrier, inc=1, device_id=(y_peer(d) * nz + z, e), device_id_type=MESH)
    pl.semaphore_signal(barrier, inc=1, device_id=(seq, partner), device_id_type=MESH)
    for d in range(1, chips):
        pl.semaphore_signal(barrier, inc=1, device_id=(seq, chip_peer(d)), device_id_type=MESH)

    def iota(shape, axis):
        return lax.broadcasted_iota(jnp.int32, shape, axis)

    def lane_of(count):
        return iota((count, LANES), 1)

    def by_head(columns):
        count = columns[0].shape[0]
        lane = lax.rem(lane_of(count), heads)
        spread = jnp.broadcast_to(columns[0], (count, LANES))
        for h in range(1, heads):
            spread = jnp.where(lane == h, columns[h], spread)
        return spread

    def thirds(values):
        high = values.astype(BF16).astype(F32)
        rest = values - high
        middle = rest.astype(BF16).astype(F32)
        return high, middle, rest - middle

    def pack_stats(top, total):
        group = lax.div(lane_of(top.shape[0]), heads)
        high, middle, low = thirds(top)
        total_high = total.astype(BF16).astype(F32)
        packed = jnp.where(group == 0, high, total - total_high)
        packed = jnp.where(group == 1, middle, packed)
        packed = jnp.where(group == 2, low, packed)
        packed = jnp.where(group == 3, total_high, packed)
        return packed

    def stat(values, group, h):
        lane = qcols + group * heads + h
        return values[..., lane : lane + 1]

    def unpack(values, h):
        top = (stat(values, 0, h) + stat(values, 1, h)) + stat(values, 2, h)
        total = stat(values, 3, h) + stat(values, 4, h)
        return top, total, values[..., h * HEAD_DIM : (h + 1) * HEAD_DIM]

    def column(row):
        size = row.shape[1]
        on = iota((size, size), 0) == iota((size, size), 1)
        return jnp.sum(jnp.where(on, row, 0.0), axis=1, keepdims=True)

    tok = tok_ref[...].astype(F32)
    ones = jnp.ones((width, LANES), F32)
    normed = (tok * column(gains_ref[0:1, :])).astype(BF16)
    second_gain = column(gains_ref[1:2, :])
    q_part = dot(normed, qw_ref[...], FIRST)
    kv_weight = kvw_ref[...].astype(F32)
    k_part = dot(normed, kv_weight[:, 0, :].astype(BF16), FIRST)
    v_part = dot(normed, kv_weight[:, 1, :].astype(BF16), FIRST)
    squares = dot(tok * tok, ones, FIRST, HIGHEST)
    for part in range(ny):
        here = slice(part * ry, (part + 1) * ry)
        a_sy[part, :, 0:qcols] = q_part[here].astype(BF16)
        a_sy[part, :, qcols:kcols] = k_part[here].astype(BF16)
        a_sy[part, :, kcols:vcols] = v_part[here].astype(BF16)
        a_sy[part, :, vcols : vcols + LANES] = squares[here].astype(BF16)

    pl.semaphore_wait(barrier, (ny - 1) + (nz - 1) + chips)
    copies = y_exchange(a_sy, a_ry, 0)

    owners = []
    for p in range(blocks):
        place, start, owner = place_ref[p], 0, -1
        for r in range(requests):
            owner = owner + (place >= start).astype(jnp.int32)
            start = start + count_ref[r]
        owners.append(owner)
    same = [[(owners[p] == owners[q]).astype(jnp.int32) for q in range(blocks)] for p in range(blocks)]
    select, leads = [], []
    step = iota((8, rows), 0)
    wanted = iota((8, rows), 1)
    for p in range(blocks):
        chosen = (wanted == owners[p] + step * requests) & (step < steps)
        chosen = jnp.where(chosen, 1.0, 0.0)
        select.append(chosen)
        first = 1
        for q in range(p):
            first = first * (1 - same[p][q])
        leads.append(chosen * first.astype(F32) if p else chosen)
    select = jnp.concatenate(select, axis=0).astype(BF16)
    leads = jnp.concatenate(leads, axis=0).astype(BF16)

    part_sum = summed(a_sy[y], a_ry, copies)
    a_sz[...] = part_sum.reshape(nz, rp, part_sum.shape[1]).astype(BF16)
    copies = z_exchange(a_sz, a_rz, 0)
    arrive(copies)
    fresh = a_sz[z].astype(F32) + jnp.sum(a_rz[...].astype(F32), axis=0)
    attn_rms = lax.rsqrt(fresh[:, vcols : vcols + 1] / depth + EPSILON)
    own = (fresh[:, 0:vcols] * attn_rms).astype(BF16)
    a_g[y, z] = own
    gather(a_g, 1)
    fresh_rows = a_g[...].astype(F32).reshape(rows, vcols)[:, 0:qcols].astype(BF16)

    picked = dot(select, fresh_rows, MIDDLE)
    tops, totals, sums = [], [], []
    for p in range(blocks):
        here = slice(p * 8, (p + 1) * 8)
        block_query = jnp.concatenate(
            [picked[here, h * HEAD_DIM : (h + 1) * HEAD_DIM] for h in range(heads)], axis=0
        )
        scores = dot(block_query.astype(BF16), cache_ref[0, p], LAST) * scale
        top = jnp.max(scores, axis=1, keepdims=True)
        weights = jnp.exp(scores - top).astype(BF16)
        total = jnp.sum(weights.astype(F32), axis=1, keepdims=True)
        weighted = dot(weights, cache_ref[1, p], MIDDLE)
        alive = live_ref[p].astype(F32)
        top = by_head([top[h * 8 : (h + 1) * 8] for h in range(heads)])
        tops.append(top * alive + (1.0 - alive) * NEGATIVE)
        totals.append(by_head([total[h * 8 : (h + 1) * 8] for h in range(heads)]) * alive)
        sums.append(weighted * alive)
    joint, joint_sums = [], []
    for p in range(blocks):
        best = tops[p]
        for q in range(blocks):
            if q != p:
                apart = (1 - same[p][q]).astype(F32) * NEGATIVE
                best = jnp.maximum(best, tops[q] + apart)
        factor = jnp.exp(tops[p] - best)
        joint.append(best)
        joint_sums.append(
            jnp.concatenate(
                [sums[p][h * 8 : (h + 1) * 8] * factor[:, h : h + 1] for h in range(heads)]
                + [totals[p] * factor],
                axis=1,
            )
        )
    joint_sums = jnp.concatenate(joint_sums, axis=0)
    sums_high = joint_sums.astype(BF16)
    sums_low = (joint_sums - sums_high.astype(F32)).astype(BF16)
    local = dot(select, sums_high, FIRST) + dot(select, sums_low, FIRST)
    joint = jnp.concatenate(joint, axis=0)
    joint = jnp.where(lane_of(joint.shape[0]) < LANES // 2, joint, 1.0)
    local_top = sum(dot(leads, third.astype(BF16), FIRST) for third in reversed(thirds(joint)))
    present = local_top[:, LANES - 1 : LANES] > 0.5
    local_top = jnp.where(present, local_top, NEGATIVE)
    local_stats = pack_stats(local_top, local[:, qcols : qcols + LANES]).astype(BF16)
    for part in range(ny):
        here = slice(part * ry, (part + 1) * ry)
        e_sy[part, :, 0:qcols] = local[here, 0:qcols].astype(BF16)
        e_sy[part, :, qcols : qcols + LANES] = local_stats[here]
    copies = y_exchange(e_sy, e_ry, 2)

    own = own.astype(F32)
    new_rows = [a_g[s, z].astype(F32) for s in range(steps)]
    fresh_parts = []
    for h in range(heads):
        query = own[:, h * HEAD_DIM : (h + 1) * HEAD_DIM]
        scores = []
        for s in range(steps):
            score = jnp.sum(query * new_rows[s][:, qcols:kcols], axis=1, keepdims=True) * scale
            scores.append(jnp.where(y >= s, score, NEGATIVE))
        new_top = functools.reduce(jnp.maximum, scores)
        new_total, new_sum = 0.0, 0.0
        for s in range(steps):
            weight = jnp.where(y >= s, jnp.exp(scores[s] - new_top), 0.0)
            weight = weight.astype(BF16).astype(F32)
            new_total = new_total + weight
            new_sum = new_sum + weight * new_rows[s][:, kcols:vcols]
        fresh_parts.append((new_top, new_total, new_sum))

    arrive(copies)
    parts = [e_sy[y].astype(F32)] + [e_ry[slot].astype(F32) for slot in range(ny - 1)]
    tops, totals = [], []
    for h in range(heads):
        pieces = [unpack(values, h) for values in parts]
        top = functools.reduce(jnp.maximum, [piece[0] for piece in pieces])
        total, weighted = 0.0, 0.0
        for piece in pieces:
            factor = jnp.exp(piece[0] - top)
            total = total + factor * piece[1]
            weighted = weighted + factor * piece[2]
        tops.append(top)
        totals.append(total)
        e_sz[:, :, h * HEAD_DIM : (h + 1) * HEAD_DIM] = weighted.reshape(nz, rp, HEAD_DIM).astype(BF16)
    stats = pack_stats(by_head(tops), by_head(totals))
    e_sz[:, :, qcols : qcols + LANES] = stats.reshape(nz, rp, LANES).astype(BF16)
    copies = z_exchange(e_sz, e_rz, 2)
    arrive(copies)
    values = e_rz[...].astype(F32)
    mine = e_sz[z].astype(F32)
    attended = []
    for h in range(heads):
        tops, totals, sums = unpack(values, h)
        my_top, my_total, my_sum = unpack(mine, h)
        new_top, new_total, new_sum = fresh_parts[h]
        joined = jnp.maximum(jnp.maximum(jnp.max(tops, axis=0), my_top), new_top)
        factors = jnp.exp(tops - joined[None])
        my_factor = jnp.exp(my_top - joined)
        new_factor = jnp.exp(new_top - joined)
        total = jnp.sum(factors * totals, axis=0) + my_total * my_factor + new_total * new_factor
        weighted = jnp.sum(factors * sums, axis=0) + my_sum * my_factor + new_sum * new_factor
        attended.append(weighted / total)
    e_g[y, z] = jnp.concatenate(attended, axis=1).astype(BF16)
    gather(e_g, 3)
    attention = e_g[...].astype(F32).reshape(rows, qcols).astype(BF16)

    head_part = dot(ow_ref[...], attention, LAST)
    residual = tok + x_reduce(head_part, 0)

    hidden = (residual * second_gain).astype(BF16)
    hidden_float = hidden.astype(F32)
    router = jnp.concatenate(
        [router_ref[...].astype(F32), jnp.zeros((LANES - experts, width), F32)], axis=0
    ).astype(BF16)
    logits = dot(hidden, router, (((0,), (1,)), ((), ())))
    squares = dot(residual * residual, ones, FIRST, HIGHEST)
    stats = jnp.where(lane_of(rows) < experts, logits, squares).astype(BF16)
    for part in range(ny):
        s_sy[part] = stats[part * ry : (part + 1) * ry]
    stat_copies = y_exchange(s_sy, s_ry, 4)
    chunks = [(k, c) for k in range(TOPK) for c in range(2)]
    masked = [None] * TOPK
    y_copies, z_copies = [], []

    def pass_on(j):
        part_sum = summed(b_sy[j, y], b_ry.at[j], y_copies[j])
        b_sz[j] = part_sum.reshape(nz, rp, ff).astype(BF16)
        z_copies.append(z_exchange(b_sz.at[j], b_rz.at[j], 5 + j))

    for j, (k, c) in enumerate(chunks):
        if c == 0:
            masked = jnp.concatenate(
                [
                    jnp.where(routes_ref[k : k + 1, :] == expert, hidden_float, 0.0)
                    for expert in range(experts)
                ],
                axis=0,
            ).astype(BF16)
        product = dot(masked, ein_ref[:, c].reshape(experts * width, ff), FIRST)
        for part in range(ny):
            b_sy[j, part] = product[part * ry : (part + 1) * ry].astype(BF16)
        y_copies.append(y_exchange(b_sy.at[j], b_ry.at[j], 5 + j))
        if j == 0:
            part_sum = summed(s_sy[y], s_ry, stat_copies)
            s_sz[...] = part_sum.reshape(nz, rp, LANES).astype(BF16)
            stat_copies = z_exchange(s_sz, s_rz, 4)
        if j >= 2:
            pass_on(j - 2)
    pass_on(2)
    pass_on(3)
    arrive(stat_copies)
    stats = s_sz[z].astype(F32) + jnp.sum(s_rz[...].astype(F32), axis=0)
    moe_rms = lax.rsqrt(stats[:, LANES // 2 : LANES // 2 + 1] / depth + EPSILON)
    sigmoids = []
    for k in range(TOPK):
        wanted = jnp.full((rp, LANES), route_ref[k, seq * rp], jnp.int32)
        for row in range(1, rp):
            wanted = jnp.where(iota((rp, LANES), 0) == row, route_ref[k, seq * rp + row], wanted)
        logit = jnp.sum(jnp.where(lane_of(rp) == wanted, stats, 0.0), axis=1, keepdims=True) * moe_rms
        sigmoids.append(1.0 / (1.0 + jnp.exp(-logit)))
    z_held = []
    for k in range(TOPK):
        pair = []
        for c in range(2):
            j = 2 * k + c
            arrive(z_copies[j])
            pair.append((b_sz[j, z].astype(F32) + jnp.sum(b_rz[j].astype(F32), axis=0)) * moe_rms)
        active = pair[0] / (1.0 + jnp.exp(-pair[0])) * pair[1]
        b_g[k, y, z] = (active * (sigmoids[k] / (sigmoids[0] + sigmoids[1]))).astype(BF16)
        z_held.append(z_gather(b_g.at[k], 9 + k))
    y_held = []
    for k in range(TOPK):
        arrive(z_held[k])
        y_held.append(y_gather(b_g.at[k], 9 + k))
    expert_part = jnp.zeros(residual.shape, F32)
    for k in range(TOPK):
        arrive(y_held[k])
        active = b_g[k].astype(F32).reshape(rows, ff).astype(BF16)
        product = dot(eout_ref[...].reshape(experts * width, ff), active, LAST)
        for expert in range(experts):
            expert_part = expert_part + jnp.where(
                routes_ref[k : k + 1, :] == expert,
                product[expert * width : (expert + 1) * width],
                0.0,
            )
    out_ref[...] = (residual + x_reduce(expert_part, 1)).astype(BF16)
    for copy in started:
        copy.wait_send()


def per_device(
    nx,
    seq_size,
    tokens,
    norm_gains,
    q_weight,
    kv_weight,
    out_weight,
    kv_cache,
    block_count,
    placement,
    block_live,
    router_weight,
    routes,
    expert_in,
    expert_out,
):
    width, rows = tokens.shape
    steps = rows // block_count.shape[0]
    ny, nz = steps, seq_size // steps
    rp = rows // seq_size
    ff = expert_in.shape[3]
    qcols = q_weight.shape[1]
    vcols = qcols + 2 * HEAD_DIM
    acols, ecols = vcols + LANES, qcols + LANES
    ry = rows // ny
    chunks = 2 * TOPK
    phases = 7 + chunks
    vmem = pl.BlockSpec(memory_space=pltpu.VMEM)
    smem = pl.BlockSpec(memory_space=pltpu.SMEM)
    return pl.pallas_call(
        functools.partial(kernel, (ny, nz, nx, width * seq_size, steps)),
        out_shape=jax.ShapeDtypeStruct((width, rows), BF16),
        in_specs=[smem] * 4 + [vmem] * 10,
        out_specs=vmem,
        scratch_shapes=[
            pltpu.VMEM((ny, ry, acols), BF16),
            pltpu.VMEM((ny - 1, ry, acols), BF16),
            pltpu.VMEM((nz, rp, acols), BF16),
            pltpu.VMEM((nz - 1, rp, acols), BF16),
            pltpu.VMEM((ny, nz, rp, vcols), BF16),
            pltpu.VMEM((ny, ry, ecols), BF16),
            pltpu.VMEM((ny - 1, ry, ecols), BF16),
            pltpu.VMEM((nz, rp, ecols), BF16),
            pltpu.VMEM((nz - 1, rp, ecols), BF16),
            pltpu.VMEM((ny, nz, rp, qcols), BF16),
            pltpu.VMEM((ny, ry, LANES), BF16),
            pltpu.VMEM((ny - 1, ry, LANES), BF16),
            pltpu.VMEM((nz, rp, LANES), BF16),
            pltpu.VMEM((nz - 1, rp, LANES), BF16),
            pltpu.VMEM((chunks, ny, ry, ff), BF16),
            pltpu.VMEM((chunks, ny - 1, ry, ff), BF16),
            pltpu.VMEM((chunks, nz, rp, ff), BF16),
            pltpu.VMEM((chunks, nz - 1, rp, ff), BF16),
            pltpu.VMEM((TOPK, ny, nz, rp, ff), BF16),
            pltpu.VMEM((2, 2, width, rows), BF16),
            pltpu.VMEM((2, width, rows), BF16),
            pltpu.VMEM((2, nx // 2, width, rows), BF16),
            pltpu.SemaphoreType.DMA((phases, ny - 1)),
            pltpu.SemaphoreType.DMA((phases, nz - 1)),
            pltpu.SemaphoreType.DMA((2, nx // 2)),
            pltpu.SemaphoreType.DMA((phases, ny - 1)),
            pltpu.SemaphoreType.DMA((phases, nz - 1)),
            pltpu.SemaphoreType.DMA((2, nx // 2)),
        ],
        compiler_params=pltpu.CompilerParams(
            collective_id=0, has_side_effects=True, vmem_limit_bytes=60 * 1024 * 1024
        ),
    )(
        block_count,
        placement,
        block_live,
        routes.T,
        tokens,
        norm_gains,
        q_weight,
        kv_weight,
        out_weight,
        kv_cache,
        router_weight.T,
        routes.T,
        expert_in,
        expert_out,
    )


def solution(mesh):
    return jax.shard_map(
        functools.partial(per_device, mesh.shape["exp"], mesh.shape["seq"]),
        mesh=mesh,
        in_specs=(
            P("seq", None),
            P(None, "seq"),
            P("seq", "exp"),
            P("seq", None, "exp"),
            P("seq", "exp"),
            P(None, "seq", None, "exp"),
            P(),
            P("seq"),
            P("seq"),
            P("seq", None),
            P(),
            P(None, None, "seq", "exp"),
            P(None, "seq", "exp"),
        ),
        out_specs=P("seq", None),
        check_vma=False,
    )
```

time: 132 us -> 115 us (0.87)
  local copies, waits for them, and re-layouts: 7.91 us -> 1.32 us
  Pallas kernels: 119 us -> 114 us
  other arithmetic: 4.7 us -> 0 us
    pallas_call x1, Pallas kernels: 119 us -> 114 us  [per_device(): pl.pallas_call(functools.partial(kernel, (ny, nz, nx, width * seq_size, s...]
    unnamed x4 -> x1, local copies, waits for them, and re-layouts: 4.83 us -> 1.32 us
    convert_element_type x3 -> x0, other arithmetic: 2.69 us -> none  [the longest x1 1.14 us: per_device(): alive = (block_live == 1).astype(F32)]
where the time goes in v2:
time: 115 us
  Pallas kernels  114 us (99%)
  local copies, waits for them, and re-layouts  1.32 us (1%)
    pallas_call x1, Pallas kernels, per_device(): pl.pallas_call(functools.partial(kernel, (ny, nz, nx, width * seq_size, s...  114 us

profile of v2, /device:TPU:1, one launch (start us, length us, event | category | flops | bytes accessed | tf_op | source)
XLA Modules:
  0.0 115.0 jit_solution(17772105903289205180)
XLA Ops:
  0.0 113.7 %shard_map.127 = bf16[64,128]{1,0:T(8,128)(2,1)} custom-call(s32[32]{0:T(128)} %count_ref.1, s32[8]{0:T(128)} %place_ref.1, s32[8]{0:T(128)} %live_ref.1, s32[2,128]{1,0:T(2,128)} %bitcast.2, bf16[64,128]{1,0:T(8,128)(2,1)} %tok_ref.1, f32[2,64]{1,0:T(2,128)} %gains_ref.1, bf16[64,512]{1,0:T(8,128)(2,1)} %qw_ref.1, bf16[64,2,128]{2,1,0:T(2,128)(2,1)} %kvw_ref.1, ...), custom_call_target="tpu_custom_call" | custom-call | tf_op jit(solution)/shard_map/pallas_call | solution.py:509
  113.7 1.3 %copy.15 = bf16[64,128]{1,0:T(8,128)(2,1)} copy(bf16[64,128]{1,0:T(8,128)(2,1)} %shard_map.127) | data formatting | bytes 32768

commit v3 on v2

--- a/solution.py
+++ b/solution.py
@@ -43,11 +43,11 @@
     qw_ref,
     kvw_ref,
     ow_ref,
-    cache_ref,
+    cache_hbm,
     router_ref,
     routes_ref,
-    ein_ref,
-    eout_ref,
+    ein_hbm,
+    eout_hbm,
     out_ref,
     a_sy,
     a_ry,
@@ -77,6 +77,10 @@
     y_recv,
     z_recv,
     x_recv,
+    cache_ref,
+    ein_ref,
+    eout_ref,
+    load_sem,
 ):
     ny, nz, nx, depth, steps = cfg
     width, rows = tok_ref.shape
@@ -140,15 +144,35 @@
     def z_exchange(send, recv, phase):
         return [z_push(send.at[z_peer(d)], recv.at[d - 1], d, phase) for d in ring_order(nz)]
 
+    def y_copy(src, d, phase):
+        return pltpu.make_async_remote_copy(
+            src_ref=src,
+            dst_ref=src,
+            send_sem=y_send.at[phase, d - 1],
+            recv_sem=y_recv.at[phase, d - 1],
+            device_id=(y_peer(d) * nz + z, e),
+            device_id_type=MESH,
+        )
+
+    def forward(held, slot, phase):
+        for d in ring_order(ny):
+            y_copy(held.at[y, slot], d, phase).start()
+
     def z_gather(held, phase):
-        return [z_push(held.at[y, z], held.at[y, z], d, phase) for d in ring_order(nz)]
-
-    def y_gather(held, phase):
-        return [y_push(held.at[y], held.at[y], d, phase) for d in ring_order(ny)]
+        copies = [z_push(held.at[y, z], held.at[y, z], d, phase) for d in ring_order(nz)]
+        forward(held, z, phase)
+        return copies
+
+    def y_gather(held, phase, copies):
+        for d, copy in reversed(list(zip(ring_order(nz), copies))):
+            copy.wait_recv()
+            forward(held, lax.rem(z + nz - d, nz), phase)
+        whole = [y_copy(held.at[y], d, phase) for d in ring_order(ny)]
+        started.extend(whole)
+        return whole
 
     def gather(held, phase):
-        arrive(z_gather(held, phase))
-        arrive(y_gather(held, phase))
+        arrive(y_gather(held, phase, z_gather(held, phase)))
 
     def summed(own, recv, copies):
         total = own.astype(F32)
@@ -237,6 +261,14 @@
         on = iota((size, size), 0) == iota((size, size), 1)
         return jnp.sum(jnp.where(on, row, 0.0), axis=1, keepdims=True)
 
+    loads = [
+        pltpu.make_async_copy(cache_hbm, cache_ref, load_sem.at[0]),
+        pltpu.make_async_copy(ein_hbm, ein_ref, load_sem.at[1]),
+        pltpu.make_async_copy(eout_hbm, eout_ref, load_sem.at[2]),
+    ]
+    for load in loads:
+        load.start()
+
     tok = tok_ref[...].astype(F32)
     ones = jnp.ones((width, LANES), F32)
     normed = (tok * column(gains_ref[0:1, :])).astype(BF16)
@@ -290,6 +322,7 @@
     fresh_rows = a_g[...].astype(F32).reshape(rows, vcols)[:, 0:qcols].astype(BF16)
 
     picked = dot(select, fresh_rows, MIDDLE)
+    loads[0].wait()
     tops, totals, sums = [], [], []
     for p in range(blocks):
         here = slice(p * 8, (p + 1) * 8)
@@ -406,6 +439,7 @@
     for part in range(ny):
         s_sy[part] = stats[part * ry : (part + 1) * ry]
     stat_copies = y_exchange(s_sy, s_ry, 4)
+    loads[1].wait()
     chunks = [(k, c) for k in range(TOPK) for c in range(2)]
     masked = [None] * TOPK
     y_copies, z_copies = [], []
@@ -458,8 +492,8 @@
         z_held.append(z_gather(b_g.at[k], 9 + k))
     y_held = []
     for k in range(TOPK):
-        arrive(z_held[k])
-        y_held.append(y_gather(b_g.at[k], 9 + k))
+        y_held.append(y_gather(b_g.at[k], 9 + k, z_held[k]))
+    loads[2].wait()
     expert_part = jnp.zeros(residual.shape, F32)
     for k in range(TOPK):
         arrive(y_held[k])
@@ -506,10 +540,11 @@
     phases = 7 + chunks
     vmem = pl.BlockSpec(memory_space=pltpu.VMEM)
     smem = pl.BlockSpec(memory_space=pltpu.SMEM)
+    held = pl.BlockSpec(memory_space=pl.ANY)
     return pl.pallas_call(
         functools.partial(kernel, (ny, nz, nx, width * seq_size, steps)),
         out_shape=jax.ShapeDtypeStruct((width, rows), BF16),
-        in_specs=[smem] * 4 + [vmem] * 10,
+        in_specs=[smem] * 4 + [vmem] * 5 + [held, vmem, vmem, held, held],
         out_specs=vmem,
         scratch_shapes=[
             pltpu.VMEM((ny, ry, acols), BF16),
@@ -540,6 +575,10 @@
             pltpu.SemaphoreType.DMA((phases, ny - 1)),
             pltpu.SemaphoreType.DMA((phases, nz - 1)),
             pltpu.SemaphoreType.DMA((2, nx // 2)),
+            pltpu.VMEM(kv_cache.shape, BF16),
+            pltpu.VMEM(expert_in.shape, BF16),
+            pltpu.VMEM(expert_out.shape, BF16),
+            pltpu.SemaphoreType.DMA((3,)),
         ],
         compiler_params=pltpu.CompilerParams(
             collective_id=0, has_side_effects=True, vmem_limit_bytes=60 * 1024 * 1024

time: 115 us -> 112 us (0.974)
  Pallas kernels: 114 us -> 110 us
    pallas_call x1, Pallas kernels: 114 us -> 110 us  [per_device(): pl.pallas_call(functools.partial(kernel, (ny, nz, nx, width * seq_size, s...]
where the time goes in v3:
time: 112 us; the launch traced here: 111 us
  Pallas kernels  110 us (98%)
  local copies, waits for them, and re-layouts  1.32 us (1%)
    pallas_call x1, Pallas kernels, per_device(): pl.pallas_call(functools.partial(kernel, (ny, nz, nx, width * seq_size, s...  110 us

profile of v3, /device:TPU:1, one launch (start us, length us, event | category | flops | bytes accessed | tf_op | source)
XLA Modules:
  0.0 111.4 jit_solution(4601114984880878706)
XLA Ops:
  0.0 110.1 %shard_map.127 = bf16[64,128]{1,0:T(8,128)(2,1)} custom-call(s32[32]{0:T(128)} %count_ref.1, s32[8]{0:T(128)} %place_ref.1, s32[8]{0:T(128)} %live_ref.1, s32[2,128]{1,0:T(2,128)} %bitcast.2, bf16[64,128]{1,0:T(8,128)(2,1)} %tok_ref.1, f32[2,64]{1,0:T(2,128)} %gains_ref.1, bf16[64,512]{1,0:T(8,128)(2,1)} %qw_ref.1, bf16[64,2,128]{2,1,0:T(2,128)(2,1)} %kvw_ref.1, ...), custom_call_target="tpu_custom_call" | custom-call | tf_op jit(solution)/shard_map/pallas_call | solution.py:544
  110.1 1.3 %copy.15 = bf16[64,128]{1,0:T(8,128)(2,1)} copy(bf16[64,128]{1,0:T(8,128)(2,1)} %shard_map.127) | data formatting | bytes 32768

commit v4 on v3

--- a/solution.py
+++ b/solution.py
@@ -430,15 +430,6 @@
 
     hidden = (residual * second_gain).astype(BF16)
     hidden_float = hidden.astype(F32)
-    router = jnp.concatenate(
-        [router_ref[...].astype(F32), jnp.zeros((LANES - experts, width), F32)], axis=0
-    ).astype(BF16)
-    logits = dot(hidden, router, (((0,), (1,)), ((), ())))
-    squares = dot(residual * residual, ones, FIRST, HIGHEST)
-    stats = jnp.where(lane_of(rows) < experts, logits, squares).astype(BF16)
-    for part in range(ny):
-        s_sy[part] = stats[part * ry : (part + 1) * ry]
-    stat_copies = y_exchange(s_sy, s_ry, 4)
     loads[1].wait()
     chunks = [(k, c) for k in range(TOPK) for c in range(2)]
     masked = [None] * TOPK
@@ -463,6 +454,16 @@
             b_sy[j, part] = product[part * ry : (part + 1) * ry].astype(BF16)
         y_copies.append(y_exchange(b_sy.at[j], b_ry.at[j], 5 + j))
         if j == 0:
+            router = jnp.concatenate(
+                [router_ref[...].astype(F32), jnp.zeros((LANES - experts, width), F32)], axis=0
+            ).astype(BF16)
+            logits = dot(hidden, router, (((0,), (1,)), ((), ())))
+            squares = dot(residual * residual, ones, FIRST, HIGHEST)
+            stats = jnp.where(lane_of(rows) < experts, logits, squares).astype(BF16)
+            for part in range(ny):
+                s_sy[part] = stats[part * ry : (part + 1) * ry]
+            stat_copies = y_exchange(s_sy, s_ry, 4)
+        if j == 1:
             part_sum = summed(s_sy[y], s_ry, stat_copies)
             s_sz[...] = part_sum.reshape(nz, rp, LANES).astype(BF16)
             stat_copies = z_exchange(s_sz, s_rz, 4)

time: 112 us -> 112 us (level)
  no operation moved by 1% of the time
where the time goes in v4:
time: 112 us
  Pallas kernels  111 us (99%)
  local copies, waits for them, and re-layouts  1.32 us (1%)
    pallas_call x1, Pallas kernels, per_device(): pl.pallas_call(functools.partial(kernel, (ny, nz, nx, width * seq_size, s...  111 us

profile of v4, /device:TPU:1, one launch (start us, length us, event | category | flops | bytes accessed | tf_op | source)
XLA Modules:
  0.0 112.3 jit_solution(14532936819128662219)
XLA Ops:
  0.0 110.9 %shard_map.127 = bf16[64,128]{1,0:T(8,128)(2,1)} custom-call(s32[32]{0:T(128)} %count_ref.1, s32[8]{0:T(128)} %place_ref.1, s32[8]{0:T(128)} %live_ref.1, s32[2,128]{1,0:T(2,128)} %bitcast.2, bf16[64,128]{1,0:T(8,128)(2,1)} %tok_ref.1, f32[2,64]{1,0:T(2,128)} %gains_ref.1, bf16[64,512]{1,0:T(8,128)(2,1)} %qw_ref.1, bf16[64,2,128]{2,1,0:T(2,128)(2,1)} %kvw_ref.1, ...), custom_call_target="tpu_custom_call" | custom-call | tf_op jit(solution)/shard_map/pallas_call | solution.py:545
  110.9 1.3 %copy.15 = bf16[64,128]{1,0:T(8,128)(2,1)} copy(bf16[64,128]{1,0:T(8,128)(2,1)} %shard_map.127) | data formatting | bytes 32768
